TPU v7x, 512 devices: a whole 4x8x8 slice. The times are simulated.
512 devices in a mesh: src: 32 (over x, y_lo, core), rcv: 16 (over z, y_hi).
Axes of the slice: x: 4, y: 8 (y_hi: 2, y_lo: 4; y = y_hi * 4 + y_lo), z: 8, core: 2. Of those that a mesh axis runs over, the one named last changes fastest.
Arguments:
- traces: float32 [2, 2, 4096, 8192], P(None, None, 'src', 'rcv'), may hold values from -6 to 6
- tap_table: float32 [8, 2, 2, 15, 64], replicated, may hold values from -1 to 1
- receiver_bins: int32 [8, 8192], replicated, may hold values from 0 to 63
- source_bins: int32 [8, 4096], replicated, may hold values from 0 to 63
Outputs:
- redatumed: float32 [2, 2, 16, 512, 4096], P(None, None, 'rcv', 'src')
All inputs are finite; a program needn't handle non-finite values.
Results may differ from a plain program's by a relative error of at most 0.0002.
Values sent between devices are 32-bit elements; how exact they have to be, the bound alone decides.
No kernel may reach another device: no remote copies, remote signals or barrier semaphores. Data moves between devices by JAX's collectives and lax.ppermute only.
A program may use at most 192 MiB of HBM per device.

v0:
```python
import functools

import jax
import jax.numpy as jnp
from jax import lax
from jax.experimental import pallas as pl
from jax.experimental.pallas import tpu as pltpu
from jax.sharding import PartitionSpec as P

F = 2
TAPS = 15
BINS = 64
STEPS = 8
HALF = 7
MARGIN = HALF * STEPS
TILE = 512
S_DEV = 128
GROUPS = 32
PER = 16
NSRC = GROUPS * S_DEV
OUTS = 112
WIN = 128
BLOCKS = 6
ROWS = 704
PCOLS = 768
RUN = 32
KINDS = 3
TROWS = 48
BF16 = jnp.bfloat16
F32 = jnp.float32
MIB = 1024 * 1024


def choose(quarter, pieces):
    out = pieces[3]
    for q in range(3):
        out = jnp.where(quarter == q, pieces[q], out)
    return out


def turned(x, shift):
    shift %= 128
    return x if shift == 0 else pltpu.roll(x, shift, axis=1)


def prepare_kernel(
    tile_ref,
    bins_ref,
    table_ref,
    local_ref,
    source_ref,
    out_ref,
    turned0_ref,
    turned1_ref,
    ordered_ref,
    split_ref,
    tiles,
):
    rows = lax.broadcasted_iota(jnp.int32, (BINS, PCOLS), 0)
    lanes = lax.broadcasted_iota(jnp.int32, (1, PCOLS), 1)
    tile = tile_ref[0]
    total = bins_ref.shape[1]
    start = tile * TILE
    before = pl.multiple_of(jnp.maximum(start - 128, 0), 128)
    after = pl.multiple_of(jnp.minimum(start + TILE, total - 128), 128)
    window = jnp.concatenate(
        [
            jnp.where(tile > 0, bins_ref[:, pl.ds(before, 128)], -1),
            bins_ref[:, pl.ds(pl.multiple_of(start, TILE), TILE)],
            jnp.where(start + TILE < total, bins_ref[:, pl.ds(after, 128)], -1),
        ],
        axis=1,
    )
    blank = jnp.zeros((1, BINS), F32)
    for d in range(STEPS):
        offset = 128 - MARGIN + HALF * (d + 1)
        row = pltpu.roll(window[d : d + 1, :], PCOLS - offset, axis=1)
        count = TILE + 2 * MARGIN - 2 * HALF * (d + 1)
        row = jnp.where(lanes < count, row, -1)
        onehot = jnp.where(rows == row, 1.0, 0.0).astype(BF16)
        parts = []
        for f in range(F):
            pair = [jnp.concatenate([table_ref[d, c, f], blank], axis=0) for c in range(2)]
            his = [x.astype(BF16) for x in pair]
            parts += his + [(x - h.astype(F32)).astype(BF16) for x, h in zip(pair, his)]
        table = jnp.concatenate(parts, axis=0)
        taps = jnp.dot(table, onehot, preferred_element_type=F32)
        for start in range(0, BLOCKS * OUTS, 128):
            size = min(128, BLOCKS * OUTS - start)
            piece = taps[:, start : start + 128].T
            out_ref[d, start : start + size, :] = piece[:size].astype(BF16)
    for f in range(F):
        for c in range(2):
            for i in range(TILE // 128):
                at = slice(i * 128, (i + 1) * 128)
                (turned0_ref, turned1_ref)[f][c, at, :] = local_ref[c, f, :, at].T
    quarter = lax.broadcasted_iota(jnp.int32, (RUN, 128), 1) // 32
    for i in range(GROUPS):
        tiles[i * 8 : (i + 1) * 8, :] = source_ref[:, i * 128 : (i + 1) * 128]
    for half in range(2):
        four = [tiles[pl.ds(4 * half + r, GROUPS, stride=8), :] for r in range(4)]
        t = jnp.concatenate(four, axis=0).T
        for r in range(4):
            pieces = [turned(t[32 * q : 32 * q + 32], 32 * (q - r)) for q in range(4)]
            ordered_ref[4 * half + r] = choose(quarter, pieces)
    unused = jnp.zeros((TROWS, 256 - 3 * BINS), BF16)
    for d in range(STEPS):
        for f in range(F):
            re, im = table_ref[d, 0, f], table_ref[d, 1, f]
            full = jnp.concatenate([re, blank, im - re, blank, re + im, blank], axis=0)
            hi = full.astype(BF16)
            rest = full - hi.astype(F32)
            mid = rest.astype(BF16)
            lo = (rest - mid.astype(F32)).astype(BF16)
            split_ref[f, d] = jnp.concatenate([hi, mid, lo, unused], axis=1)


def prepare(tile, bins, table, local, source_bins):
    vmem = pl.BlockSpec(memory_space=pltpu.VMEM)
    return pl.pallas_call(
        prepare_kernel,
        out_shape=(
            pltpu.VMEM((STEPS, BLOCKS * OUTS, 128), BF16),
            pltpu.VMEM((2, TILE, S_DEV), F32),
            pltpu.VMEM((2, TILE, S_DEV), F32),
            pltpu.HBM((STEPS, RUN, 128), jnp.int32),
            pltpu.HBM((F, STEPS, TROWS, 256), BF16),
        ),
        in_specs=[pl.BlockSpec(memory_space=pltpu.SMEM)] + [vmem] * 4,
        out_specs=(vmem,) * 5,
        scratch_shapes=[pltpu.VMEM((GROUPS * 8, 128), jnp.int32)],
        compiler_params=pltpu.CompilerParams(vmem_limit_bytes=10 * MIB),
        cost_estimate=pl.CostEstimate(flops=200_000_000, bytes_accessed=3_200_000, transcendentals=0),
        name="prepare",
    )(tile, bins, table, local, source_bins)


def put_split(dst, c, start, size, value):
    hi = value.astype(BF16)
    dst[c, start : start + size, 0:128] = hi
    dst[c, start : start + size, 128:256] = (value - hi.astype(F32)).astype(BF16)


def rcv_kernel(f, local_ref, low_ref, high_ref, taps_ref, *rest):
    out_ref, first, za, zb, last = rest[-5:]
    for c in range(2):
        first[0:MARGIN, :] = low_ref[c, f]
        first[MARGIN : MARGIN + TILE, :] = local_ref[c]
        first[MARGIN + TILE : 2 * MARGIN + TILE, :] = high_ref[c, f]
        first[2 * MARGIN + TILE :, :] = jnp.zeros((ROWS - 2 * MARGIN - TILE, 128), F32)
        for base in range(0, ROWS, 64):
            put_split(za, c, base, 64, first[base : base + 64, :])
        zb[c, BLOCKS * OUTS :, :] = jnp.zeros((ROWS - BLOCKS * OUTS, 256), BF16)

    p = lax.broadcasted_iota(jnp.int32, (OUTS, 128), 0)
    lane = lax.broadcasted_iota(jnp.int32, (OUTS, 128), 1)
    band = (lane >= p) & (lane < p + TAPS)

    def unit(src, dst, d, b, keep):
        start = b * OUTS
        w = taps_ref[d, start : start + OUTS, :].astype(F32)
        parts = []
        for kind in range(4):
            shift = (256 - 64 * f - 16 * kind) % 128
            turned = pltpu.roll(w, shift, axis=1, stride=1, stride_axis=0)
            parts.append(jnp.where(band, turned, 0.0).astype(BF16))
        re_hi, im_hi, re_lo, im_lo = parts
        lhs = jnp.concatenate(
            [
                jnp.concatenate([re_hi, -im_hi], axis=1),
                jnp.concatenate([im_hi, re_hi], axis=1),
                jnp.concatenate([re_lo, -im_lo], axis=1),
                jnp.concatenate([im_lo, re_lo], axis=1),
            ],
            axis=0,
        )
        rhs = jnp.concatenate(
            [src[0, start : start + WIN, :], src[1, start : start + WIN, :]], axis=0
        )
        product = jnp.dot(lhs, rhs, preferred_element_type=F32)
        for c in range(2):
            top = product[c * OUTS : (c + 1) * OUTS]
            low = product[(2 + c) * OUTS : (3 + c) * OUTS]
            value = top[:, :128] + (top[:, 128:] + low[:, :128])
            put_split(dst, c, start, OUTS, value)
            if keep:
                last[c, start : start + OUTS, :] = value

    def two_steps(i, blocks):
        for b in range(blocks):
            unit(za, zb, 2 * i, b, False)
        for b in range(blocks):
            unit(zb, za, 2 * i + 1, b, True)

    lax.fori_loop(0, 2, lambda i, _: (two_steps(i, BLOCKS), 0)[1], 0)
    lax.fori_loop(2, 4, lambda i, _: (two_steps(i, BLOCKS - 1), 0)[1], 0)
    for c in range(2):
        for g in range(GROUPS):
            out_ref[g, c, 0] = last[c, g * PER : (g + 1) * PER, :]


def rcv_steps(f, local, low, high, taps, *tokens):
    vmem = pl.BlockSpec(memory_space=pltpu.VMEM)
    return pl.pallas_call(
        functools.partial(rcv_kernel, f),
        out_shape=pltpu.HBM((GROUPS, 2, 1, PER, S_DEV), F32),
        in_specs=[vmem] * 4 + [pl.BlockSpec(memory_space=pl.ANY)] * len(tokens),
        out_specs=vmem,
        scratch_shapes=[
            pltpu.VMEM((ROWS, 128), F32),
            pltpu.VMEM((2, ROWS, 256), BF16),
            pltpu.VMEM((2, ROWS, 256), BF16),
            pltpu.VMEM((2, BLOCKS * OUTS, 128), F32),
        ],
        compiler_params=pltpu.CompilerParams(vmem_limit_bytes=10 * MIB),
        cost_estimate=pl.CostEstimate(
            flops=2_500_000_000, bytes_accessed=4_000_000, transcendentals=0
        ),
        name="rcv_steps",
    )(local, low, high, taps, *tokens)


def look_up(dst, row_of, table, m0):
    which = lax.broadcasted_iota(jnp.int32, (BINS, 128), 0)
    halves = []
    for h in range(2):
        onehot = jnp.where(which == row_of(m0 + h), 1.0, 0.0).astype(BF16)
        halves.append(jnp.concatenate([onehot] * 3, axis=0))
    taps = jnp.dot(table, jnp.concatenate(halves, axis=1), preferred_element_type=F32)
    for h in range(2):
        dst[m0 + h] = taps[:, h * 128 : (h + 1) * 128]


def src_taps_kernel(bins_ref, table_ref, out_ref, token_ref):
    token_ref[...] = jnp.zeros_like(token_ref)
    for i in range(RUN // 2):
        look_up(
            out_ref.at[0],
            lambda m: bins_ref[0, m : m + 1, :],
            table_ref[0, 0, :, : KINDS * BINS],
            2 * i,
        )


def src_taps(f, bins, table):
    return pl.pallas_call(
        src_taps_kernel,
        grid=(STEPS,),
        out_shape=(
            pltpu.HBM((STEPS, RUN, TROWS, 128), F32),
            pltpu.HBM((8, 128), F32),
        ),
        in_specs=[
            pl.BlockSpec((1, RUN, 128), lambda d: (d, 0, 0)),
            pl.BlockSpec((1, 1, TROWS, 256), lambda d: (f, d, 0, 0)),
        ],
        out_specs=(
            pl.BlockSpec((1, RUN, TROWS, 128), lambda d: (d, 0, 0, 0)),
            pl.BlockSpec((8, 128), lambda d: (0, 0)),
        ),
        compiler_params=pltpu.CompilerParams(
            vmem_limit_bytes=8 * MIB, dimension_semantics=("arbitrary",)
        ),
        cost_estimate=pl.CostEstimate(
            flops=1_200_000_000, bytes_accessed=13_000_000, transcendentals=0
        ),
        name="src_taps",
    )(bins, table)


PAD = HALF
MROWS = RUN + 2 * PAD


MB = 2


NSCRATCH = {True: 12, False: 9}


def src_kernel(f, inline, recv_ref, bins_ref, table_ref, *rest):
    out_ref, xa, xb, swap, place, stage, sems, in_sems, *looked = rest[1 if len(rest) > NSCRATCH[inline] else 0 :]
    if inline:
        wa, wb, bins, table = looked
    else:
        (held,) = looked
        wa = wb = None

    if inline:
        first = [
            pltpu.make_async_copy(bins_ref, bins, in_sems.at[0]),
            pltpu.make_async_copy(table_ref.at[f], table, in_sems.at[1]),
        ]
    else:
        first = [
            pltpu.make_async_copy(bins_ref.at[d], held.at[d], in_sems.at[d]) for d in range(STEPS)
        ]
    for copy in first:
        copy.start()
    quarter = lax.broadcasted_iota(jnp.int32, (RUN, 128), 1) // 32
    lane = lax.broadcasted_iota(jnp.int32, (PER, 128), 1)

    def taps_of(dst, d, m0):
        look_up(
            dst, lambda m: bins[d, pl.ds(m, 1), :], table[d, :, : KINDS * BINS], m0
        )

    def put(dst, m, re, im):
        dst[0, m] = re
        dst[1, m] = im
        dst[2, m] = re + im

    def halo(x):
        for m in range(PAD):
            parts = []
            for c in range(2):
                v = x[c, RUN + m]
                one = jnp.where(lane == 0, 0.0, pltpu.roll(v, 33, axis=1))
                parts.append(jnp.where(lane < 32, one, pltpu.roll(v, 32, axis=1)))
            put(x, m, *parts)
            parts = []
            for c in range(2):
                v = x[c, PAD + m]
                one = jnp.where(lane == 127, 0.0, pltpu.roll(v, 95, axis=1))
                parts.append(jnp.where(lane >= 96, one, pltpu.roll(v, 96, axis=1)))
            put(x, PAD + RUN + m, *parts)

    for c in range(2):
        for a in range(PER // 4):
            rows = [
                recv_ref[pl.ds(c * PER + 4 * a + r, GROUPS, stride=2 * PER), :] for r in range(4)
            ]
            t = jnp.concatenate(rows, axis=0).T
            for r in range(4):
                pieces = [turned(t[32 * q : 32 * q + 32], 32 * (q - r)) for q in range(4)]
                swap[c, (4 * a + r) * RUN : (4 * a + r + 1) * RUN, :] = choose(quarter, pieces)
    for m in range(RUN):
        put(xa, PAD + m, *[swap[c, pl.ds(m, PER, stride=RUN), :] for c in range(2)])
    halo(xa)
    if inline:
        for copy in first:
            copy.wait()
        for i in range(RUN // 2):
            taps_of(wa, 0, 2 * i)

    def one_step(src, dst, now, later, d):
        if not inline:
            pltpu.make_async_copy(bins_ref.at[d], held.at[d], in_sems.at[d]).wait()
        tap_rows = now if inline else held.at[d]

        def block(i, carry):
            m0 = i * MB
            if inline:
                taps_of(later, jnp.minimum(d + 1, STEPS - 1), m0)
            seen = {}

            def load(kind, row, rt):
                key = (kind, row, rt)
                if key not in seen:
                    seen[key] = src[kind, m0 + row, rt * 8 : (rt + 1) * 8, :]
                return seen[key]

            sums = {}
            for k in range(TAPS):
                for mm in range(MB):
                    taps = [
                        tap_rows[m0 + mm, pl.ds(kind * 16 + k, 8, stride=0), :]
                        for kind in range(KINDS)
                    ]
                    for rt in range(2):
                        a = load(0, mm + k, rt)
                        b = load(1, mm + k, rt)
                        s = load(2, mm + k, rt)
                        new = [taps[0] * s, taps[1] * a, taps[2] * b]
                        old = sums.get((mm, rt))
                        sums[(mm, rt)] = new if old is None else [x + y for x, y in zip(old, new)]
            for mm in range(MB):
                for rt in range(2):
                    k1, k2, k3 = sums[(mm, rt)]
                    re = k1 - k3
                    im = k1 + k2
                    at = slice(rt * 8, (rt + 1) * 8)
                    dst[0, PAD + m0 + mm, at, :] = re
                    dst[1, PAD + m0 + mm, at, :] = im
                    dst[2, PAD + m0 + mm, at, :] = re + im
            return carry

        lax.fori_loop(0, RUN // MB, block, 0, unroll=4)

    def two_steps(i, carry):
        one_step(xa, xb, wa, wb, 2 * i)
        halo(xb)
        one_step(xb, xa, wb, wa, 2 * i + 1)
        halo(xa)
        return carry

    lax.fori_loop(0, STEPS // 2, two_steps, 0)
    copies = []
    for c in range(2):
        for m in range(RUN):
            swap[c, pl.ds(m, PER, stride=RUN), :] = xa[c, PAD + m]
        for a in range(PER // 4):
            rows = [swap[c, (4 * a + r) * RUN : (4 * a + r + 1) * RUN, :] for r in range(4)]
            t = jnp.concatenate(
                [
                    choose(quarter, [turned(rows[r], 32 * (r - q)) for r in range(4)])
                    for q in range(4)
                ],
                axis=0,
            ).T
            for r in range(4):
                at = 4 * a + r
                place[c, at // 8, pl.ds(at % 8, GROUPS, stride=8), :] = t[32 * r : 32 * r + 32]
            if a % 2:
                rt = a // 2
                for i in range(GROUPS):
                    stage[c, rt, :, i * 128 : (i + 1) * 128] = place[c, rt, i * 8 : (i + 1) * 8, :]
                copy = pltpu.make_async_copy(
                    stage.at[c, rt],
                    out_ref.at[c, f, 0, rt * 8 : (rt + 1) * 8, :],
                    sems.at[c, rt],
                )
                copy.start()
                copies.append(copy)
    for copy in copies:
        copy.wait()


def src_steps(f, inline, received, bins, table, earlier=None):
    vmem = pl.BlockSpec(memory_space=pltpu.VMEM)
    flat = received.reshape(GROUPS * 2 * PER, S_DEV)
    anywhere = pl.BlockSpec(memory_space=pl.ANY)
    hbm = pl.BlockSpec(memory_space=pltpu.HBM)
    in_specs = [vmem, hbm, hbm]
    args = [flat, bins, table]
    aliases = {}
    if earlier is not None:
        in_specs.append(pl.BlockSpec(memory_space=pl.ANY))
        args.append(earlier)
        aliases = {3: 0}
    return pl.pallas_call(
        functools.partial(src_kernel, f, inline),
        out_shape=pltpu.HBM((2, F, 1, PER, NSRC), F32),
        in_specs=in_specs,
        out_specs=pl.BlockSpec(memory_space=pl.ANY),
        scratch_shapes=[
            pltpu.VMEM((KINDS, MROWS, PER, 128), F32),
            pltpu.VMEM((KINDS, MROWS, PER, 128), F32),
            pltpu.VMEM((2, PER * RUN, 128), F32),
            pltpu.VMEM((2, 2, GROUPS * 8, 128), F32),
            pltpu.VMEM((2, 2, 8, NSRC), F32),
            pltpu.SemaphoreType.DMA((2, 2)),
            pltpu.SemaphoreType.DMA((STEPS,)),
        ]
        + (
            [
                pltpu.VMEM((RUN, TROWS, 128), F32),
                pltpu.VMEM((RUN, TROWS, 128), F32),
                pltpu.VMEM((STEPS, RUN, 128), jnp.int32),
                pltpu.VMEM((STEPS, TROWS, 256), BF16),
            ]
            if inline
            else [pltpu.VMEM((STEPS, RUN, TROWS, 128), F32)]
        ),
        input_output_aliases=aliases,
        compiler_params=pltpu.CompilerParams(vmem_limit_bytes=(20 if inline else 58) * MIB),
        cost_estimate=pl.CostEstimate(
            flops=3_000_000_000, bytes_accessed=8_000_000, transcendentals=0
        ),
        name="src_steps",
    )(*args)


def shards(traces, tap_table, receiver_bins, source_bins):
    count = lax.axis_size("rcv")
    forward = [(i, i + 1) for i in range(count - 1)]
    backward = [(target, source) for source, target in forward]
    tile = lax.axis_index("rcv").astype(jnp.int32).reshape(1)
    tail = traces[:, :, :, TILE - MARGIN :].transpose(0, 1, 3, 2)
    head = traces[:, :, :, :MARGIN].transpose(0, 1, 3, 2)
    low = lax.ppermute(tail, "rcv", forward)
    high = lax.ppermute(head, "rcv", backward)
    r_taps, *local, bins, table = prepare(tile, receiver_bins, tap_table, traces, source_bins)
    sent = rcv_steps(0, local[0], low, high, r_taps)
    bins1, sent = lax.optimization_barrier((bins, sent))
    got0 = lax.all_to_all(sent, "src", split_axis=0, concat_axis=0, tiled=True)
    taps1, token = src_taps(1, bins1, table)
    sent = rcv_steps(1, local[1], low, high, r_taps, token)
    got1 = lax.all_to_all(sent, "src", split_axis=0, concat_axis=0, tiled=True)
    out = src_steps(0, True, got0, bins, table)
    return src_steps(1, False, got1, taps1, table, out)


def solution(mesh):
    in_specs = (P(None, None, "src", "rcv"), P(), P(), P())
    out_specs = P(None, None, "rcv", "src", None)
    return jax.shard_map(shards, mesh=mesh, in_specs=in_specs, out_specs=out_specs, check_vma=False)
```

profile of v0, /device:TPU:255, one launch (start us, length us, event | category | flops | bytes accessed | tf_op | source)
XLA Modules:
  0.0 88.2 jit_solution(17794767440289824734)
XLA Ops:
  0.0 1.2 %fusion = (f32[2,2,128,56]{3,2,1,0:T(8,128)S(1)}, f32[2,2,128,56]{3,2,1,0:T(8,128)S(1)}) fusion(f32[2,2,128,512]{3,2,1,0:T(8,128)} %local_ref.1), kind=kLoop, calls=%fused_computation | loop fusion | bytes 458752 | tf_op jit(solution)/shard_map/slice | solution.py:480
  1.2 0.1 copy.9
  1.3 7.5 %collective-permute-start = (f32[2,2,56,128]{3,2,1,0:T(8,128)S(1)}, f32[2,2,56,128]{3,2,1,0:T(8,128)S(1)}, u32[]{:S(2)}, u32[]{:S(2)}) collective-permute-start(f32[2,2,56,128]{3,2,1,0:T(8,128)S(1)} %bitcast.7), channel_id=1, source_target_pairs={{0,1},{1,2},{2,3},{3,4},{4,5},{5,6},{6,7},{7,8},{8,9},{9,10},{10,1... | collective-permute-start | bytes 344072 | tf_op jit(solution)/shard_map/ppermute | solution.py:481
  8.7 0.1 copy.10
  8.9 1.9 %collective-permute-start.1 = (f32[2,2,56,128]{3,2,1,0:T(8,128)S(1)}, f32[2,2,56,128]{3,2,1,0:T(8,128)S(1)}, u32[]{:S(2)}, u32[]{:S(2)}) collective-permute-start(f32[2,2,56,128]{3,2,1,0:T(8,128)S(1)} %bitcast.8), channel_id=1, source_target_pairs={{1,0},{2,1},{3,2},{4,3},{5,4},{6,5},{7,6},{8,7},{9,8},{10,9},{11,1... | collective-permute-start | bytes 344072 | tf_op jit(solution)/shard_map/ppermute | solution.py:482
  10.8 1.0 %copy.6.table_ref = f32[8,2,2,15,64]{4,3,2,1,0:T(8,128)S(1)} copy(f32[8,2,2,15,64]{4,2,3,1,0:T(2,128)} %param.5) | data formatting | bytes 245760 | tf_op args[1]
  11.8 0.0 copy-start
  11.8 1.2 %copy-done = f32[2,2,128,512]{3,2,1,0:T(8,128)S(1)} copy-done((f32[2,2,128,512]{3,2,1,0:T(8,128)S(1)}, f32[2,2,128,512]{3,2,1,0:T(8,128)}, u32[]{:S(2)}) %copy-start) | copy-done | bytes 1048600
  13.0 0.0 copy-start.1
  13.0 0.9 %copy-done.1 = s32[8,8192]{1,0:T(8,128)S(1)} copy-done((s32[8,8192]{1,0:T(8,128)S(1)}, s32[8,8192]{1,0:T(8,128)}, u32[]{:S(2)}) %copy-start.1) | copy-done | bytes 262168
  14.0 0.0 copy-start.2
  14.0 0.9 %copy-done.2 = s32[8,4096]{1,0:T(8,128)S(1)} copy-done((s32[8,4096]{1,0:T(8,128)S(1)}, s32[8,4096]{1,0:T(8,128)}, u32[]{:S(2)}) %copy-start.2) | copy-done | bytes 131096
  14.9 2.1 %prepare.1 = (bf16[8,672,128]{2,1,0:T(8,128)(2,1)S(1)}, f32[2,512,128]{2,1,0:T(8,128)S(1)}, f32[2,512,128]{2,1,0:T(8,128)S(1)}, s32[8,32,128]{2,1,0:T(8,128)}, bf16[2,8,48,256]{3,2,1,0:T(8,128)(2,1)}) custom-call(s32[1]{0:T(128)} %bitcast.tile_ref, s32[8,8192]{1,0:T(8,128)S(1)} %copy-done.1, f32[8,2,2,15,64]{4,3,2,1,0:T(8,128)S(1)} %copy.6.table_ref, ...), custom_call_target="tpu_custom_call" | custom-call | flops 200000000 | bytes 3200000 | tf_op jit(solution)/shard_map/prepare/pallas_call | solution.py:120
  17.0 0.0 copy-start.3
  17.0 0.0 copy-start.4
  17.0 0.0 collective-permute-done.low_ref
  17.0 7.1 %collective-permute-done.1.high_ref = f32[2,2,56,128]{3,2,1,0:T(8,128)S(1)} collective-permute-done((f32[2,2,56,128]{3,2,1,0:T(8,128)S(1)}, f32[2,2,56,128]{3,2,1,0:T(8,128)S(1)}, u32[]{:S(2)}, u32[]{:S(2)}) %collective-permute-start.1) | collective-permute-done | bytes 114720 | tf_op jit(solution)/shard_map/ppermute | solution.py:482
  24.1 4.7 %rcv_steps.2 = f32[32,2,1,16,128]{4,3,2,1,0:T(8,128)} custom-call(f32[2,512,128]{2,1,0:T(8,128)S(1)} %get-tuple-element.17.local_ref, f32[2,2,56,128]{3,2,1,0:T(8,128)S(1)} %collective-permute-done.low_ref, f32[2,2,56,128]{3,2,1,0:T(8,128)S(1)} %collective-permute-done.1.high_ref, bf16[8,672,128]{2,1,0:T(8,128)(2,1)S(1)} %get-tuple-element.15.taps_ref), custom_call_target="tpu_custom_call" | custom-call | flops 2500000000 | bytes 4000000 | tf_op jit(solution)/shard_map/rcv_steps/pallas_call | solution.py:204
  28.7 8.1 %all-to-all-start.1 = ((f32[32,2,1,16,128]{4,3,2,1,0:T(8,128)}), f32[32,2,1,16,128]{4,3,2,1,0:T(8,128)S(1)}, u32[]{:S(2)}, u32[]{:S(2)}) async-start(f32[32,2,1,16,128]{4,3,2,1,0:T(8,128)} %rcv_steps.2), calls=%async_computation.1 | async-start | bytes 1048576 | tf_op jit(solution)/shard_map/all_to_all | solution.py:486
  36.8 0.0 copy-done.3
  36.8 0.0 copy-done.4
  36.8 5.6 %src_taps.1 = (f32[8,32,48,128]{3,2,1,0:T(8,128)}, f32[8,128]{1,0:T(8,128)}) custom-call(s32[8,32,128]{2,1,0:T(8,128)S(1)} %copy-done.4, bf16[2,8,48,256]{3,2,1,0:T(8,128)(2,1)S(1)} %copy-done.3), custom_call_target="tpu_custom_call" | custom-call | flops 1200000000 | bytes 13000000 | tf_op jit(solution)/shard_map/src_taps/pallas_call | solution.py:246
  42.4 0.0 copy-start.5
  42.4 0.7 copy-done.5
  43.1 4.7 %rcv_steps.3 = f32[32,2,1,16,128]{4,3,2,1,0:T(8,128)} custom-call(f32[2,512,128]{2,1,0:T(8,128)S(1)} %get-tuple-element.14.local_ref, f32[2,2,56,128]{3,2,1,0:T(8,128)S(1)} %collective-permute-done.low_ref, f32[2,2,56,128]{3,2,1,0:T(8,128)S(1)} %collective-permute-done.1.high_ref, bf16[8,672,128]{2,1,0:T(8,128)(2,1)S(1)} %get-tuple-element.15.taps_ref, ...), custom_call_target="tpu_custom_call" | custom-call | flops 2500000000 | bytes 4000000 | tf_op jit(solution)/shard_map/rcv_steps/pallas_call | solution.py:204
  47.8 2.1 %all-to-all-done.1 = f32[32,2,1,16,128]{4,3,2,1,0:T(8,128)S(1)} async-done(((f32[32,2,1,16,128]{4,3,2,1,0:T(8,128)}), f32[32,2,1,16,128]{4,3,2,1,0:T(8,128)S(1)}, u32[]{:S(2)}, u32[]{:S(2)}) %all-to-all-start.1) | async-done | bytes 524320 | tf_op jit(solution)/shard_map/all_to_all | solution.py:486
  49.9 7.4 %all-to-all-start = ((f32[32,2,1,16,128]{4,3,2,1,0:T(8,128)}), f32[32,2,1,16,128]{4,3,2,1,0:T(8,128)S(1)}, u32[]{:S(2)}, u32[]{:S(2)}) async-start(f32[32,2,1,16,128]{4,3,2,1,0:T(8,128)} %rcv_steps.3), calls=%async_computation | async-start | bytes 1048576 | tf_op jit(solution)/shard_map/all_to_all | solution.py:489
  57.3 16.9 %src_steps.2.rest_0_ = f32[2,2,1,16,4096]{4,3,2,1,0:T(8,128)} custom-call(f32[1024,128]{1,0:T(8,128)S(1)} %bitcast.5, s32[8,32,128]{2,1,0:T(8,128)S(1)} %copy-done.4, bf16[2,8,48,256]{3,2,1,0:T(8,128)(2,1)S(1)} %copy-done.3), custom_call_target="tpu_custom_call" | custom-call | flops 3000000000 | bytes 8000000 | tf_op jit(solution)/shard_map/src_steps/pallas_call | solution.py:441
  74.2 0.0 all-to-all-done
  74.2 0.0 copy-start.6
  74.2 0.8 copy-done.6
  75.0 13.0 %src_steps.3 = f32[2,2,1,16,4096]{4,3,2,1,0:T(8,128)} custom-call(f32[1024,128]{1,0:T(8,128)} %bitcast.6, f32[8,32,48,128]{3,2,1,0:T(8,128)} %get-tuple-element.21.bins_ref, bf16[2,8,48,256]{3,2,1,0:T(8,128)(2,1)} %get-tuple-element.19.table_ref, f32[2,2,1,16,4096]{4,3,2,1,0:T(8,128)} %src_steps.2.rest_0_), custom_call_target="tpu_custom_call", output_to_operand_aliasing={{}: (3, {})} | custom-call | flops 3000000000 | bytes 8000000 | tf_op jit(solution)/shard_map/src_steps/pallas_call | solution.py:441
Async XLA Ops:
  1.3 15.7 %collective-permute-start = (f32[2,2,56,128]{3,2,1,0:T(8,128)S(1)}, f32[2,2,56,128]{3,2,1,0:T(8,128)S(1)}, u32[]{:S(2)}, u32[]{:S(2)}) collective-permute-start(f32[2,2,56,128]{3,2,1,0:T(8,128)S(1)} %bitcast.7), channel_id=1, source_target_pairs={{0,1},{1,2},{2,3},{3,4},{4,5},{5,6},{6,7},{7,8},{8,9},{9,10},{10,1... | collective-permute-start | bytes 344072 | tf_op jit(solution)/shard_map/ppermute | solution.py:481
  8.9 15.2 %collective-permute-start.1 = (f32[2,2,56,128]{3,2,1,0:T(8,128)S(1)}, f32[2,2,56,128]{3,2,1,0:T(8,128)S(1)}, u32[]{:S(2)}, u32[]{:S(2)}) collective-permute-start(f32[2,2,56,128]{3,2,1,0:T(8,128)S(1)} %bitcast.8), channel_id=1, source_target_pairs={{1,0},{2,1},{3,2},{4,3},{5,4},{6,5},{7,6},{8,7},{9,8},{10,9},{11,1... | collective-permute-start | bytes 344072 | tf_op jit(solution)/shard_map/ppermute | solution.py:482
  11.8 1.2 %copy-start = (f32[2,2,128,512]{3,2,1,0:T(8,128)S(1)}, f32[2,2,128,512]{3,2,1,0:T(8,128)}, u32[]{:S(2)}) copy-start(f32[2,2,128,512]{3,2,1,0:T(8,128)} %local_ref.1) | copy-start | bytes 3145732
  13.0 0.9 %copy-start.1 = (s32[8,8192]{1,0:T(8,128)S(1)}, s32[8,8192]{1,0:T(8,128)}, u32[]{:S(2)}) copy-start(s32[8,8192]{1,0:T(8,128)} %bins_ref.1) | copy-start | bytes 786436
  14.0 0.9 %copy-start.2 = (s32[8,4096]{1,0:T(8,128)S(1)}, s32[8,4096]{1,0:T(8,128)}, u32[]{:S(2)}) copy-start(s32[8,4096]{1,0:T(8,128)} %source_ref.1) | copy-start | bytes 393220
  17.0 19.8 %copy-start.3 = (bf16[2,8,48,256]{3,2,1,0:T(8,128)(2,1)S(1)}, bf16[2,8,48,256]{3,2,1,0:T(8,128)(2,1)}, u32[]{:S(2)}) copy-start(bf16[2,8,48,256]{3,2,1,0:T(8,128)(2,1)} %get-tuple-element.19.table_ref) | copy-start | bytes 1179652
  17.0 19.8 %copy-start.4 = (s32[8,32,128]{2,1,0:T(8,128)S(1)}, s32[8,32,128]{2,1,0:T(8,128)}, u32[]{:S(2)}) copy-start(s32[8,32,128]{2,1,0:T(8,128)} %get-tuple-element.18.bins_ref) | copy-start | bytes 393220
  28.7 21.1 %all-to-all-start.1 = ((f32[32,2,1,16,128]{4,3,2,1,0:T(8,128)}), f32[32,2,1,16,128]{4,3,2,1,0:T(8,128)S(1)}, u32[]{:S(2)}, u32[]{:S(2)}) async-start(f32[32,2,1,16,128]{4,3,2,1,0:T(8,128)} %rcv_steps.2), calls=%async_computation.1 | async-start | bytes 1048576 | tf_op jit(solution)/shard_map/all_to_all | solution.py:486
  42.4 0.7 copy-start.5
  49.9 24.3 %all-to-all-start = ((f32[32,2,1,16,128]{4,3,2,1,0:T(8,128)}), f32[32,2,1,16,128]{4,3,2,1,0:T(8,128)S(1)}, u32[]{:S(2)}, u32[]{:S(2)}) async-start(f32[32,2,1,16,128]{4,3,2,1,0:T(8,128)} %rcv_steps.3), calls=%async_computation | async-start | bytes 1048576 | tf_op jit(solution)/shard_map/all_to_all | solution.py:489
  74.2 0.8 copy-start.6
where the time goes:
time: 88.7 us; the launch traced here: 88.2 us
  Pallas kernels  46.9 us (53%)
  starting transfers between devices  24.9 us (28%)
  waiting for transfers between devices  9.19 us (10%)
  local copies, waits for them, and re-layouts  6.92 us (8%)
    pallas_call x2, Pallas kernels, src_steps(): pl.pallas_call(functools.partial(src_kernel, f, inline), out_shape=pltpu....  29.9 us
    pallas_call x2, Pallas kernels, rcv_steps(): pl.pallas_call(functools.partial(rcv_kernel, f), out_shape=pltpu.HBM((GRO...  9.33 us
    all_to_all x1, starting transfers between devices, shards(): got0 = lax.all_to_all(sent, 'src', split_axis=0, concat_axis=0, tiled=True)  8.05 us
    ppermute x1, starting transfers between devices, shards(): low = lax.ppermute(tail, 'rcv', forward)  7.45 us
    all_to_all x1, starting transfers between devices, shards(): got1 = lax.all_to_all(sent, 'src', split_axis=0, concat_axis=0, tiled=True)  7.43 us
    ppermute x1, waiting for transfers between devices, shards(): high = lax.ppermute(head, 'rcv', backward)  7.09 us
    unnamed x17, local copies, waits for them, and re-layouts  5.76 us
    pallas_call x1, Pallas kernels, src_taps(): pl.pallas_call(src_taps_kernel, grid=(STEPS,), out_shape=(pltpu.HBM((STEP...  5.6 us
  transfers between devices with their start and end apart: 4, of which 2 were waited for; matrix products, arithmetic and copies ran while one was open for 1% of the time, Pallas kernels for 33%

commit v1 on v0

--- a/solution.py
+++ b/solution.py
@@ -25,6 +25,7 @@
 PCOLS = 768
 RUN = 32
 KINDS = 3
+SPARE = 5
 TROWS = 48
 BF16 = jnp.bfloat16
 F32 = jnp.float32
@@ -235,7 +236,7 @@
     token_ref[...] = jnp.zeros_like(token_ref)
     for i in range(RUN // 2):
         look_up(
-            out_ref.at[0],
+            out_ref.at[0, 0],
             lambda m: bins_ref[0, m : m + 1, :],
             table_ref[0, 0, :, : KINDS * BINS],
             2 * i,
@@ -247,7 +248,7 @@
         src_taps_kernel,
         grid=(STEPS,),
         out_shape=(
-            pltpu.HBM((STEPS, RUN, TROWS, 128), F32),
+            pltpu.HBM((SPARE, STEPS, RUN, TROWS, 128), F32),
             pltpu.HBM((8, 128), F32),
         ),
         in_specs=[
@@ -255,7 +256,7 @@
             pl.BlockSpec((1, 1, TROWS, 256), lambda d: (f, d, 0, 0)),
         ],
         out_specs=(
-            pl.BlockSpec((1, RUN, TROWS, 128), lambda d: (d, 0, 0, 0)),
+            pl.BlockSpec((1, 1, RUN, TROWS, 128), lambda d: (0, d, 0, 0, 0)),
             pl.BlockSpec((8, 128), lambda d: (0, 0)),
         ),
         compiler_params=pltpu.CompilerParams(
@@ -293,7 +294,7 @@
         ]
     else:
         first = [
-            pltpu.make_async_copy(bins_ref.at[d], held.at[d], in_sems.at[d]) for d in range(STEPS)
+            pltpu.make_async_copy(bins_ref.at[0, d], held.at[d], in_sems.at[d]) for d in range(STEPS)
         ]
     for copy in first:
         copy.start()
@@ -345,7 +346,7 @@
 
     def one_step(src, dst, now, later, d):
         if not inline:
-            pltpu.make_async_copy(bins_ref.at[d], held.at[d], in_sems.at[d]).wait()
+            pltpu.make_async_copy(bins_ref.at[0, d], held.at[d], in_sems.at[d]).wait()
         tap_rows = now if inline else held.at[d]
 
         def block(i, carry):
@@ -385,7 +386,7 @@
                     dst[2, PAD + m0 + mm, at, :] = re + im
             return carry
 
-        lax.fori_loop(0, RUN // MB, block, 0, unroll=4)
+        lax.fori_loop(0, RUN // MB, block, 0, unroll=RUN // MB)
 
     def two_steps(i, carry):
         one_step(xa, xb, wa, wb, 2 * i)
@@ -463,7 +464,7 @@
             else [pltpu.VMEM((STEPS, RUN, TROWS, 128), F32)]
         ),
         input_output_aliases=aliases,
-        compiler_params=pltpu.CompilerParams(vmem_limit_bytes=(20 if inline else 58) * MIB),
+        compiler_params=pltpu.CompilerParams(vmem_limit_bytes=(20 if inline else 36) * MIB),
         cost_estimate=pl.CostEstimate(
             flops=3_000_000_000, bytes_accessed=8_000_000, transcendentals=0
         ),

time: 88.7 us -> 84.6 us (0.954)
  the two profiles are of different devices: /device:TPU:255 before, /device:TPU:193 now
where the time goes in v1:
time: 84.6 us; the launch traced here: 84 us
  Pallas kernels  39.7 us (47%)
  starting transfers between devices  24 us (28%)
  local copies, waits for them, and re-layouts  10.8 us (13%)
  waiting for transfers between devices  9.25 us (11%)
    pallas_call x2, Pallas kernels, src_steps(): pl.pallas_call(functools.partial(src_kernel, f, inline), out_shape=pltpu....  22.7 us
    unnamed x25, local copies, waits for them, and re-layouts  9.64 us
    pallas_call x2, Pallas kernels, rcv_steps(): pl.pallas_call(functools.partial(rcv_kernel, f), out_shape=pltpu.HBM((GRO...  9.32 us
    all_to_all x1, starting transfers between devices, shards(): got0 = lax.all_to_all(sent, 'src', split_axis=0, concat_axis=0, tiled=True)  9.28 us
    ppermute x1, starting transfers between devices, shards(): low = lax.ppermute(tail, 'rcv', forward)  7.45 us
    pallas_call x1, Pallas kernels, src_taps(): pl.pallas_call(src_taps_kernel, grid=(STEPS,), out_shape=(pltpu.HBM((SPAR...  5.57 us
    all_to_all x1, starting transfers between devices, shards(): got1 = lax.all_to_all(sent, 'src', split_axis=0, concat_axis=0, tiled=True)  4.62 us
    ppermute x1, waiting for transfers between devices, shards(): high = lax.ppermute(head, 'rcv', backward)  3.27 us
  transfers between devices with their start and end apart: 4, of which 3 were waited for; matrix products, arithmetic and copies ran while one was open for 1% of the time, Pallas kernels for 29%

profile of v1, /device:TPU:193, one launch (start us, length us, event | category | flops | bytes accessed | tf_op | source)
XLA Modules:
  0.0 84.0 jit_solution(6578744928615473872)
XLA Ops:
  0.0 1.2 %fusion = (f32[2,2,128,56]{3,2,1,0:T(8,128)S(1)}, f32[2,2,128,56]{3,2,1,0:T(8,128)S(1)}) fusion(f32[2,2,128,512]{3,2,1,0:T(8,128)} %local_ref.1), kind=kLoop, calls=%fused_computation | loop fusion | bytes 458752 | tf_op jit(solution)/shard_map/slice | solution.py:481
  1.2 0.1 copy.9
  1.3 7.5 %collective-permute-start = (f32[2,2,56,128]{3,2,1,0:T(8,128)S(1)}, f32[2,2,56,128]{3,2,1,0:T(8,128)S(1)}, u32[]{:S(2)}, u32[]{:S(2)}) collective-permute-start(f32[2,2,56,128]{3,2,1,0:T(8,128)S(1)} %bitcast.7), channel_id=1, source_target_pairs={{0,1},{1,2},{2,3},{3,4},{4,5},{5,6},{6,7},{7,8},{8,9},{9,10},{10,1... | collective-permute-start | bytes 344072 | tf_op jit(solution)/shard_map/ppermute | solution.py:482
  8.7 0.1 copy.10
  8.9 2.6 %collective-permute-start.1 = (f32[2,2,56,128]{3,2,1,0:T(8,128)S(1)}, f32[2,2,56,128]{3,2,1,0:T(8,128)S(1)}, u32[]{:S(2)}, u32[]{:S(2)}) collective-permute-start(f32[2,2,56,128]{3,2,1,0:T(8,128)S(1)} %bitcast.8), channel_id=1, source_target_pairs={{1,0},{2,1},{3,2},{4,3},{5,4},{6,5},{7,6},{8,7},{9,8},{10,9},{11,1... | collective-permute-start | bytes 344072 | tf_op jit(solution)/shard_map/ppermute | solution.py:483
  11.5 1.0 %copy.6.table_ref = f32[8,2,2,15,64]{4,3,2,1,0:T(8,128)S(1)} copy(f32[8,2,2,15,64]{4,2,3,1,0:T(2,128)} %param.5) | data formatting | bytes 245760 | tf_op args[1]
  12.5 0.0 copy-start
  12.5 1.2 %copy-done = f32[2,2,128,512]{3,2,1,0:T(8,128)S(1)} copy-done((f32[2,2,128,512]{3,2,1,0:T(8,128)S(1)}, f32[2,2,128,512]{3,2,1,0:T(8,128)}, u32[]{:S(2)}) %copy-start) | copy-done | bytes 1048600
  13.7 0.0 copy-start.4
  13.7 0.9 %copy-done.4 = s32[8,8192]{1,0:T(8,128)S(1)} copy-done((s32[8,8192]{1,0:T(8,128)S(1)}, s32[8,8192]{1,0:T(8,128)}, u32[]{:S(2)}) %copy-start.4) | copy-done | bytes 262168
  14.7 0.0 copy-start.5
  14.7 0.9 %copy-done.5 = s32[8,4096]{1,0:T(8,128)S(1)} copy-done((s32[8,4096]{1,0:T(8,128)S(1)}, s32[8,4096]{1,0:T(8,128)}, u32[]{:S(2)}) %copy-start.5) | copy-done | bytes 131096
  15.6 2.1 %prepare.1 = (bf16[8,672,128]{2,1,0:T(8,128)(2,1)S(1)}, f32[2,512,128]{2,1,0:T(8,128)S(1)}, f32[2,512,128]{2,1,0:T(8,128)S(1)}, s32[8,32,128]{2,1,0:T(8,128)}, bf16[2,8,48,256]{3,2,1,0:T(8,128)(2,1)}) custom-call(s32[1]{0:T(128)} %bitcast.tile_ref, s32[8,8192]{1,0:T(8,128)S(1)} %copy-done.4, f32[8,2,2,15,64]{4,3,2,1,0:T(8,128)S(1)} %copy.6.table_ref, ...), custom_call_target="tpu_custom_call" | custom-call | flops 200000000 | bytes 3200000 | tf_op jit(solution)/shard_map/prepare/pallas_call | solution.py:121
  17.7 0.0 copy-start.3
  17.7 0.0 collective-permute-done.low_ref
  17.7 3.3 %collective-permute-done.1.high_ref = f32[2,2,56,128]{3,2,1,0:T(8,128)S(1)} collective-permute-done((f32[2,2,56,128]{3,2,1,0:T(8,128)S(1)}, f32[2,2,56,128]{3,2,1,0:T(8,128)S(1)}, u32[]{:S(2)}, u32[]{:S(2)}) %collective-permute-start.1) | collective-permute-done | bytes 114720 | tf_op jit(solution)/shard_map/ppermute | solution.py:483
  21.0 0.0 copy-start.8
  21.0 4.7 %rcv_steps.2 = f32[32,2,1,16,128]{4,3,2,1,0:T(8,128)} custom-call(f32[2,512,128]{2,1,0:T(8,128)S(1)} %get-tuple-element.17.local_ref, f32[2,2,56,128]{3,2,1,0:T(8,128)S(1)} %collective-permute-done.low_ref, f32[2,2,56,128]{3,2,1,0:T(8,128)S(1)} %collective-permute-done.1.high_ref, bf16[8,672,128]{2,1,0:T(8,128)(2,1)S(1)} %get-tuple-element.15.taps_ref), custom_call_target="tpu_custom_call" | custom-call | flops 2500000000 | bytes 4000000 | tf_op jit(solution)/shard_map/rcv_steps/pallas_call | solution.py:205
  25.6 0.0 copy-done.8
  25.6 9.3 %all-to-all-start.1 = ((f32[32,2,1,16,128]{4,3,2,1,0:T(8,128)}), f32[32,2,1,16,128]{4,3,2,1,0:T(8,128)S(1)}, u32[]{:S(2)}, u32[]{:S(2)}) async-start(f32[32,2,1,16,128]{4,3,2,1,0:T(8,128)} %rcv_steps.2), calls=%async_computation.1 | async-start | bytes 1048576 | tf_op jit(solution)/shard_map/all_to_all | solution.py:487
  34.9 0.0 copy-start.1
  34.9 1.0 %copy-done.1 = bf16[2,8,48,256]{3,2,1,0:T(8,128)(2,1)S(1)} copy-done((bf16[2,8,48,256]{3,2,1,0:T(8,128)(2,1)S(1)}, bf16[2,8,48,256]{3,2,1,0:T(8,128)(2,1)}, u32[]{:S(2)}) %copy-start.1) | copy-done | bytes 393240
  35.9 0.0 copy-start.6
  35.9 0.9 %copy-done.6 = s32[8,32,128]{2,1,0:T(8,128)S(1)} copy-done((s32[8,32,128]{2,1,0:T(8,128)S(1)}, s32[8,32,128]{2,1,0:T(8,128)}, u32[]{:S(2)}) %copy-start.6) | copy-done | bytes 131096
  36.8 5.6 %src_taps.1 = (f32[5,8,32,48,128]{4,3,2,1,0:T(8,128)}, f32[8,128]{1,0:T(8,128)}) custom-call(s32[8,32,128]{2,1,0:T(8,128)S(1)} %copy-done.6, bf16[2,8,48,256]{3,2,1,0:T(8,128)(2,1)S(1)} %copy-done.1), custom_call_target="tpu_custom_call" | custom-call | flops 1200000000 | bytes 13000000 | tf_op jit(solution)/shard_map/src_taps/pallas_call | solution.py:247
  42.4 0.0 copy-start.9
  42.4 0.9 %copy-done.9 = f32[2,2,56,128]{3,2,1,0:T(8,128)S(1)} copy-done((f32[2,2,56,128]{3,2,1,0:T(8,128)S(1)}, f32[2,2,56,128]{3,2,1,0:T(8,128)}, u32[]{:S(2)}) %copy-start.9) | copy-done | bytes 114712
  43.3 0.0 copy-start.10
  43.3 0.7 copy-done.10
  44.0 4.7 %rcv_steps.3 = f32[32,2,1,16,128]{4,3,2,1,0:T(8,128)} custom-call(f32[2,512,128]{2,1,0:T(8,128)S(1)} %get-tuple-element.14.local_ref, f32[2,2,56,128]{3,2,1,0:T(8,128)S(1)} %collective-permute-done.low_ref, f32[2,2,56,128]{3,2,1,0:T(8,128)S(1)} %copy-done.9, bf16[8,672,128]{2,1,0:T(8,128)(2,1)S(1)} %get-tuple-element.15.taps_ref, f32[8,128]{1,0:T(8,128)S(1)} %copy-done.10), custom_call_target="tpu_custom_call" | custom-call | flops 2500000000 | bytes 4000000 | tf_op jit(solution)/shard_map/rcv_steps/pallas_call | solution.py:205
  48.6 3.1 %all-to-all-done.1 = f32[32,2,1,16,128]{4,3,2,1,0:T(8,128)S(1)} async-done(((f32[32,2,1,16,128]{4,3,2,1,0:T(8,128)}), f32[32,2,1,16,128]{4,3,2,1,0:T(8,128)S(1)}, u32[]{:S(2)}, u32[]{:S(2)}) %all-to-all-start.1) | async-done | bytes 524320 | tf_op jit(solution)/shard_map/all_to_all | solution.py:487
  51.7 4.6 %all-to-all-start = ((f32[32,2,1,16,128]{4,3,2,1,0:T(8,128)}), f32[32,2,1,16,128]{4,3,2,1,0:T(8,128)S(1)}, u32[]{:S(2)}, u32[]{:S(2)}) async-start(f32[32,2,1,16,128]{4,3,2,1,0:T(8,128)} %rcv_steps.3), calls=%async_computation | async-start | bytes 1048576 | tf_op jit(solution)/shard_map/all_to_all | solution.py:490
  56.3 0.0 copy-start.2
  56.3 1.0 %copy-done.2 = bf16[2,8,48,256]{3,2,1,0:T(8,128)(2,1)S(1)} copy-done((bf16[2,8,48,256]{3,2,1,0:T(8,128)(2,1)S(1)}, bf16[2,8,48,256]{3,2,1,0:T(8,128)(2,1)}, u32[]{:S(2)}) %copy-start.2) | copy-done | bytes 393240
  57.3 0.0 copy-start.7
  57.3 0.9 %copy-done.7 = s32[8,32,128]{2,1,0:T(8,128)S(1)} copy-done((s32[8,32,128]{2,1,0:T(8,128)S(1)}, s32[8,32,128]{2,1,0:T(8,128)}, u32[]{:S(2)}) %copy-start.7) | copy-done | bytes 131096
  58.2 12.0 %src_steps.2.rest_0_ = f32[2,2,1,16,4096]{4,3,2,1,0:T(8,128)} custom-call(f32[1024,128]{1,0:T(8,128)S(1)} %bitcast.6, s32[8,32,128]{2,1,0:T(8,128)S(1)} %copy-done.7, bf16[2,8,48,256]{3,2,1,0:T(8,128)(2,1)S(1)} %copy-done.2), custom_call_target="tpu_custom_call" | custom-call | flops 3000000000 | bytes 8000000 | tf_op jit(solution)/shard_map/src_steps/pallas_call | solution.py:442
  70.2 2.9 %all-to-all-done = f32[32,2,1,16,128]{4,3,2,1,0:T(8,128)S(1)} async-done(((f32[32,2,1,16,128]{4,3,2,1,0:T(8,128)}), f32[32,2,1,16,128]{4,3,2,1,0:T(8,128)S(1)}, u32[]{:S(2)}, u32[]{:S(2)}) %all-to-all-start) | async-done | bytes 524320 | tf_op jit(solution)/shard_map/all_to_all | solution.py:490
  73.1 0.0 copy-done.3
  73.1 10.7 %src_steps.3 = f32[2,2,1,16,4096]{4,3,2,1,0:T(8,128)} custom-call(f32[1024,128]{1,0:T(8,128)S(1)} %bitcast.5, f32[5,8,32,48,128]{4,3,2,1,0:T(8,128)} %get-tuple-element.21.bins_ref, bf16[2,8,48,256]{3,2,1,0:T(8,128)(2,1)S(1)} %copy-done.3, f32[2,2,1,16,4096]{4,3,2,1,0:T(8,128)} %src_steps.2.rest_0_), custom_call_target="tpu_custom_call", output_to_operand_aliasing={{}: (3, {})} | custom-call | flops 3000000000 | bytes 8000000 | tf_op jit(solution)/shard_map/src_steps/pallas_call | solution.py:442
Async XLA Ops:
  1.3 16.4 %collective-permute-start = (f32[2,2,56,128]{3,2,1,0:T(8,128)S(1)}, f32[2,2,56,128]{3,2,1,0:T(8,128)S(1)}, u32[]{:S(2)}, u32[]{:S(2)}) collective-permute-start(f32[2,2,56,128]{3,2,1,0:T(8,128)S(1)} %bitcast.7), channel_id=1, source_target_pairs={{0,1},{1,2},{2,3},{3,4},{4,5},{5,6},{6,7},{7,8},{8,9},{9,10},{10,1... | collective-permute-start | bytes 344072 | tf_op jit(solution)/shard_map/ppermute | solution.py:482
  8.9 12.1 %collective-permute-start.1 = (f32[2,2,56,128]{3,2,1,0:T(8,128)S(1)}, f32[2,2,56,128]{3,2,1,0:T(8,128)S(1)}, u32[]{:S(2)}, u32[]{:S(2)}) collective-permute-start(f32[2,2,56,128]{3,2,1,0:T(8,128)S(1)} %bitcast.8), channel_id=1, source_target_pairs={{1,0},{2,1},{3,2},{4,3},{5,4},{6,5},{7,6},{8,7},{9,8},{10,9},{11,1... | collective-permute-start | bytes 344072 | tf_op jit(solution)/shard_map/ppermute | solution.py:483
  12.5 1.2 %copy-start = (f32[2,2,128,512]{3,2,1,0:T(8,128)S(1)}, f32[2,2,128,512]{3,2,1,0:T(8,128)}, u32[]{:S(2)}) copy-start(f32[2,2,128,512]{3,2,1,0:T(8,128)} %local_ref.1) | copy-start | bytes 3145732
  13.7 0.9 %copy-start.4 = (s32[8,8192]{1,0:T(8,128)S(1)}, s32[8,8192]{1,0:T(8,128)}, u32[]{:S(2)}) copy-start(s32[8,8192]{1,0:T(8,128)} %bins_ref.1) | copy-start | bytes 786436
  14.7 0.9 %copy-start.5 = (s32[8,4096]{1,0:T(8,128)S(1)}, s32[8,4096]{1,0:T(8,128)}, u32[]{:S(2)}) copy-start(s32[8,4096]{1,0:T(8,128)} %source_ref.1) | copy-start | bytes 393220
  17.7 55.4 %copy-start.3 = (bf16[2,8,48,256]{3,2,1,0:T(8,128)(2,1)S(1)}, bf16[2,8,48,256]{3,2,1,0:T(8,128)(2,1)}, u32[]{:S(2)}) copy-start(bf16[2,8,48,256]{3,2,1,0:T(8,128)(2,1)} %get-tuple-element.19.table_ref) | copy-start | bytes 1179652
  21.0 4.7 %copy-start.8 = (f32[2,2,56,128]{3,2,1,0:T(8,128)}, f32[2,2,56,128]{3,2,1,0:T(8,128)S(1)}, u32[]{:S(2)}) copy-start(f32[2,2,56,128]{3,2,1,0:T(8,128)S(1)} %collective-permute-done.1.high_ref) | copy-start | bytes 344068
  25.6 26.1 %all-to-all-start.1 = ((f32[32,2,1,16,128]{4,3,2,1,0:T(8,128)}), f32[32,2,1,16,128]{4,3,2,1,0:T(8,128)S(1)}, u32[]{:S(2)}, u32[]{:S(2)}) async-start(f32[32,2,1,16,128]{4,3,2,1,0:T(8,128)} %rcv_steps.2), calls=%async_computation.1 | async-start | bytes 1048576 | tf_op jit(solution)/shard_map/all_to_all | solution.py:487
  34.9 1.0 %copy-start.1 = (bf16[2,8,48,256]{3,2,1,0:T(8,128)(2,1)S(1)}, bf16[2,8,48,256]{3,2,1,0:T(8,128)(2,1)}, u32[]{:S(2)}) copy-start(bf16[2,8,48,256]{3,2,1,0:T(8,128)(2,1)} %get-tuple-element.19.table_ref) | copy-start | bytes 1179652
  35.9 0.9 %copy-start.6 = (s32[8,32,128]{2,1,0:T(8,128)S(1)}, s32[8,32,128]{2,1,0:T(8,128)}, u32[]{:S(2)}) copy-start(s32[8,32,128]{2,1,0:T(8,128)} %get-tuple-element.18.bins_ref) | copy-start | bytes 393220
  42.4 0.9 %copy-start.9 = (f32[2,2,56,128]{3,2,1,0:T(8,128)S(1)}, f32[2,2,56,128]{3,2,1,0:T(8,128)}, u32[]{:S(2)}) copy-start(f32[2,2,56,128]{3,2,1,0:T(8,128)} %copy-done.8) | copy-start | bytes 344068
  43.3 0.7 copy-start.10
  51.7 21.4 %all-to-all-start = ((f32[32,2,1,16,128]{4,3,2,1,0:T(8,128)}), f32[32,2,1,16,128]{4,3,2,1,0:T(8,128)S(1)}, u32[]{:S(2)}, u32[]{:S(2)}) async-start(f32[32,2,1,16,128]{4,3,2,1,0:T(8,128)} %rcv_steps.3), calls=%async_computation | async-start | bytes 1048576 | tf_op jit(solution)/shard_map/all_to_all | solution.py:490
  56.3 1.0 %copy-start.2 = (bf16[2,8,48,256]{3,2,1,0:T(8,128)(2,1)S(1)}, bf16[2,8,48,256]{3,2,1,0:T(8,128)(2,1)}, u32[]{:S(2)}) copy-start(bf16[2,8,48,256]{3,2,1,0:T(8,128)(2,1)} %get-tuple-element.19.table_ref) | copy-start | bytes 1179652
  57.3 0.9 %copy-start.7 = (s32[8,32,128]{2,1,0:T(8,128)S(1)}, s32[8,32,128]{2,1,0:T(8,128)}, u32[]{:S(2)}) copy-start(s32[8,32,128]{2,1,0:T(8,128)} %get-tuple-element.18.bins_ref) | copy-start | bytes 393220

commit v2 on v1

--- a/solution.py
+++ b/solution.py
@@ -130,7 +130,7 @@
         in_specs=[pl.BlockSpec(memory_space=pltpu.SMEM)] + [vmem] * 4,
         out_specs=(vmem,) * 5,
         scratch_shapes=[pltpu.VMEM((GROUPS * 8, 128), jnp.int32)],
-        compiler_params=pltpu.CompilerParams(vmem_limit_bytes=10 * MIB),
+        compiler_params=pltpu.CompilerParams(vmem_limit_bytes=60 * MIB),
         cost_estimate=pl.CostEstimate(flops=200_000_000, bytes_accessed=3_200_000, transcendentals=0),
         name="prepare",
     )(tile, bins, table, local, source_bins)
@@ -142,29 +142,26 @@
     dst[c, start : start + size, 128:256] = (value - hi.astype(F32)).astype(BF16)
 
 
-def rcv_kernel(f, local_ref, low_ref, high_ref, taps_ref, *rest):
-    out_ref, first, za, zb, last = rest[-5:]
-    for c in range(2):
-        first[0:MARGIN, :] = low_ref[c, f]
-        first[MARGIN : MARGIN + TILE, :] = local_ref[c]
-        first[MARGIN + TILE : 2 * MARGIN + TILE, :] = high_ref[c, f]
-        first[2 * MARGIN + TILE :, :] = jnp.zeros((ROWS - 2 * MARGIN - TILE, 128), F32)
-        for base in range(0, ROWS, 64):
-            put_split(za, c, base, 64, first[base : base + 64, :])
-        zb[c, BLOCKS * OUTS :, :] = jnp.zeros((ROWS - BLOCKS * OUTS, 256), BF16)
-
+FULL = (tuple(range(BLOCKS)), tuple(range(BLOCKS - 1)))
+EDGES = ((0, 1, 4, 5), (0, 4))
+INNER = (tuple(range(5)), tuple(range(4)))
+INNER_FIRST = 64
+INNER_OUTS = TILE - MARGIN - INNER_FIRST
+
+
+def rcv_run(f, blocks, offset, taps_ref, za, zb, last):
     p = lax.broadcasted_iota(jnp.int32, (OUTS, 128), 0)
     lane = lax.broadcasted_iota(jnp.int32, (OUTS, 128), 1)
     band = (lane >= p) & (lane < p + TAPS)
 
     def unit(src, dst, d, b, keep):
         start = b * OUTS
-        w = taps_ref[d, start : start + OUTS, :].astype(F32)
+        w = taps_ref[d, offset + start : offset + start + OUTS, :].astype(F32)
         parts = []
         for kind in range(4):
             shift = (256 - 64 * f - 16 * kind) % 128
-            turned = pltpu.roll(w, shift, axis=1, stride=1, stride_axis=0)
-            parts.append(jnp.where(band, turned, 0.0).astype(BF16))
+            skewed = pltpu.roll(w, shift, axis=1, stride=1, stride_axis=0)
+            parts.append(jnp.where(band, skewed, 0.0).astype(BF16))
         re_hi, im_hi, re_lo, im_lo = parts
         lhs = jnp.concatenate(
             [
@@ -187,25 +184,89 @@
             if keep:
                 last[c, start : start + OUTS, :] = value
 
-    def two_steps(i, blocks):
-        for b in range(blocks):
+    def two_steps(i, chosen):
+        for b in chosen:
             unit(za, zb, 2 * i, b, False)
-        for b in range(blocks):
+        for b in chosen:
             unit(zb, za, 2 * i + 1, b, True)
 
-    lax.fori_loop(0, 2, lambda i, _: (two_steps(i, BLOCKS), 0)[1], 0)
-    lax.fori_loop(2, 4, lambda i, _: (two_steps(i, BLOCKS - 1), 0)[1], 0)
+    lax.fori_loop(0, 2, lambda i, _: (two_steps(i, blocks[0]), 0)[1], 0)
+    lax.fori_loop(2, 4, lambda i, _: (two_steps(i, blocks[1]), 0)[1], 0)
+
+
+def rcv_kernel(f, blocks, local_ref, low_ref, high_ref, taps_ref, *rest):
+    out_ref, first, za, zb, last = rest[-5:]
     for c in range(2):
-        for g in range(GROUPS):
-            out_ref[g, c, 0] = last[c, g * PER : (g + 1) * PER, :]
-
-
-def rcv_steps(f, local, low, high, taps, *tokens):
+        first[0:MARGIN, :] = low_ref[c, f]
+        first[MARGIN : MARGIN + TILE, :] = local_ref[c]
+        first[MARGIN + TILE : 2 * MARGIN + TILE, :] = high_ref[c, f]
+        first[2 * MARGIN + TILE :, :] = jnp.zeros((ROWS - 2 * MARGIN - TILE, 128), F32)
+        for base in range(0, ROWS, 64):
+            put_split(za, c, base, 64, first[base : base + 64, :])
+        zb[c, BLOCKS * OUTS :, :] = jnp.zeros((ROWS - BLOCKS * OUTS, 256), BF16)
+        if blocks == EDGES:
+            zb[c, 2 * OUTS : 2 * OUTS + 16, :] = jnp.zeros((16, 256), BF16)
+    rcv_run(f, blocks, 0, taps_ref, za, zb, last)
+    for c in range(2):
+        for g in range(2 * GROUPS):
+            r = g * 8
+            at = slice(r % PER, r % PER + 8)
+            if blocks == EDGES and INNER_FIRST <= r < INNER_FIRST + INNER_OUTS:
+                piece = rest[0][c, r - INNER_FIRST : r - INNER_FIRST + 8, :]
+            else:
+                piece = last[c, r : r + 8, :]
+            out_ref[r // PER, c, 0, at, :] = piece
+
+
+def inner_kernel(f, local_ref, taps_ref, out_ref, za, zb, last):
+    size = 5 * OUTS + 16
+    held = TILE - 8
+    for c in range(2):
+        for base in range(0, size, 48):
+            if base + 48 <= held:
+                value = local_ref[c, 8 + base : 8 + base + 48, :]
+            elif base < held:
+                value = jnp.concatenate(
+                    [local_ref[c, 8 + base : TILE, :], jnp.zeros((base + 48 - held, 128), F32)],
+                    axis=0,
+                )
+            else:
+                value = jnp.zeros((48, 128), F32)
+            put_split(za, c, base, 48, value)
+        zb[c, 5 * OUTS :, :] = jnp.zeros((16, 256), BF16)
+    rcv_run(f, INNER, INNER_FIRST, taps_ref, za, zb, last)
+    for c in range(2):
+        out_ref[c] = last[c, :INNER_OUTS, :]
+
+
+def rcv_inner(f, local, taps):
     vmem = pl.BlockSpec(memory_space=pltpu.VMEM)
+    size = 5 * OUTS + 16
     return pl.pallas_call(
-        functools.partial(rcv_kernel, f),
+        functools.partial(inner_kernel, f),
+        out_shape=pltpu.VMEM((2, INNER_OUTS, S_DEV), F32),
+        in_specs=[vmem, vmem],
+        out_specs=vmem,
+        scratch_shapes=[
+            pltpu.VMEM((2, size, 256), BF16),
+            pltpu.VMEM((2, size, 256), BF16),
+            pltpu.VMEM((2, 5 * OUTS, 128), F32),
+        ],
+        compiler_params=pltpu.CompilerParams(vmem_limit_bytes=10 * MIB),
+        cost_estimate=pl.CostEstimate(
+            flops=2_000_000_000, bytes_accessed=3_000_000, transcendentals=0
+        ),
+        name="rcv_inner",
+    )(local, taps)
+
+
+def rcv_steps(f, blocks, local, low, high, taps, *extra):
+    vmem = pl.BlockSpec(memory_space=pltpu.VMEM)
+    extra_spec = vmem if blocks == EDGES else pl.BlockSpec(memory_space=pl.ANY)
+    return pl.pallas_call(
+        functools.partial(rcv_kernel, f, blocks),
         out_shape=pltpu.HBM((GROUPS, 2, 1, PER, S_DEV), F32),
-        in_specs=[vmem] * 4 + [pl.BlockSpec(memory_space=pl.ANY)] * len(tokens),
+        in_specs=[vmem] * 4 + [extra_spec] * len(extra),
         out_specs=vmem,
         scratch_shapes=[
             pltpu.VMEM((ROWS, 128), F32),
@@ -218,7 +279,7 @@
             flops=2_500_000_000, bytes_accessed=4_000_000, transcendentals=0
         ),
         name="rcv_steps",
-    )(local, low, high, taps, *tokens)
+    )(local, low, high, taps, *extra)
 
 
 def look_up(dst, row_of, table, m0):
@@ -482,11 +543,12 @@
     low = lax.ppermute(tail, "rcv", forward)
     high = lax.ppermute(head, "rcv", backward)
     r_taps, *local, bins, table = prepare(tile, receiver_bins, tap_table, traces, source_bins)
-    sent = rcv_steps(0, local[0], low, high, r_taps)
+    inner = rcv_inner(0, local[0], r_taps)
+    sent = rcv_steps(0, EDGES, local[0], low, high, r_taps, inner)
     bins1, sent = lax.optimization_barrier((bins, sent))
     got0 = lax.all_to_all(sent, "src", split_axis=0, concat_axis=0, tiled=True)
     taps1, token = src_taps(1, bins1, table)
-    sent = rcv_steps(1, local[1], low, high, r_taps, token)
+    sent = rcv_steps(1, FULL, local[1], low, high, r_taps, token)
     got1 = lax.all_to_all(sent, "src", split_axis=0, concat_axis=0, tiled=True)
     out = src_steps(0, True, got0, bins, table)
     return src_steps(1, False, got1, taps1, table, out)

time: 84.6 us -> 82.7 us (0.978)
  the two profiles are of different devices: /device:TPU:193 before, /device:TPU:257 now
where the time goes in v2:
time: 82.7 us; the launch traced here: 82.2 us
  Pallas kernels  43.8 us (53%)
  starting transfers between devices  23 us (28%)
  waiting for transfers between devices  9.47 us (11%)
  local copies, waits for them, and re-layouts  5.65 us (7%)
    pallas_call x2, Pallas kernels, src_steps(): pl.pallas_call(functools.partial(src_kernel, f, inline), out_shape=pltpu....  22.7 us
    pallas_call x2, Pallas kernels, rcv_steps(): pl.pallas_call(functools.partial(rcv_kernel, f, blocks), out_shape=pltpu....  8.37 us
    all_to_all x1, starting transfers between devices, shards(): got0 = lax.all_to_all(sent, 'src', split_axis=0, concat_axis=0, tiled=True)  7.87 us
    ppermute x1, starting transfers between devices, shards(): low = lax.ppermute(tail, 'rcv', forward)  7.45 us
    pallas_call x1, Pallas kernels, src_taps(): pl.pallas_call(src_taps_kernel, grid=(STEPS,), out_shape=(pltpu.HBM((SPAR...  5.55 us
    all_to_all x1, waiting for transfers between devices, shards(): got1 = lax.all_to_all(sent, 'src', split_axis=0, concat_axis=0, tiled=True)  4.6 us
    unnamed x13, local copies, waits for them, and re-layouts  4.49 us
    all_to_all x1, waiting for transfers between devices, shards(): got0 = lax.all_to_all(sent, 'src', split_axis=0, concat_axis=0, tiled=True)  3.99 us
  transfers between devices with their start and end apart: 4, of which 3 were waited for; matrix products, arithmetic and copies ran while one was open for 2% of the time, Pallas kernels for 36%

profile of v2, /device:TPU:257, one launch (start us, length us, event | category | flops | bytes accessed | tf_op | source)
XLA Modules:
  0.0 82.2 jit_solution(10911684250361207792)
XLA Ops:
  0.0 1.2 %fusion = (f32[2,2,128,56]{3,2,1,0:T(8,128)S(1)}, f32[2,2,128,56]{3,2,1,0:T(8,128)S(1)}) fusion(f32[2,2,128,512]{3,2,1,0:T(8,128)} %local_ref.1), kind=kLoop, calls=%fused_computation | loop fusion | bytes 458752 | tf_op jit(solution)/shard_map/slice | solution.py:542
  1.2 0.1 copy.9
  1.3 7.5 %collective-permute-start = (f32[2,2,56,128]{3,2,1,0:T(8,128)S(1)}, f32[2,2,56,128]{3,2,1,0:T(8,128)S(1)}, u32[]{:S(2)}, u32[]{:S(2)}) collective-permute-start(f32[2,2,56,128]{3,2,1,0:T(8,128)S(1)} %bitcast.7), channel_id=1, source_target_pairs={{0,1},{1,2},{2,3},{3,4},{4,5},{5,6},{6,7},{7,8},{8,9},{9,10},{10,1... | collective-permute-start | bytes 344072 | tf_op jit(solution)/shard_map/ppermute | solution.py:543
  8.7 0.1 copy.10
  8.9 3.8 %collective-permute-start.1 = (f32[2,2,56,128]{3,2,1,0:T(8,128)S(1)}, f32[2,2,56,128]{3,2,1,0:T(8,128)S(1)}, u32[]{:S(2)}, u32[]{:S(2)}) collective-permute-start(f32[2,2,56,128]{3,2,1,0:T(8,128)S(1)} %bitcast.8), channel_id=1, source_target_pairs={{1,0},{2,1},{3,2},{4,3},{5,4},{6,5},{7,6},{8,7},{9,8},{10,9},{11,1... | collective-permute-start | bytes 344072 | tf_op jit(solution)/shard_map/ppermute | solution.py:544
  12.7 1.7 %copy.6.table_ref = f32[8,2,2,15,64]{4,3,2,1,0:T(8,128)} copy(f32[8,2,2,15,64]{4,2,3,1,0:T(2,128)} %param.5) | data formatting | bytes 245760 | tf_op args[1]
  14.4 3.5 %prepare.1 = (bf16[8,672,128]{2,1,0:T(8,128)(2,1)S(1)}, f32[2,512,128]{2,1,0:T(8,128)S(1)}, f32[2,512,128]{2,1,0:T(8,128)S(1)}, s32[8,32,128]{2,1,0:T(8,128)}, bf16[2,8,48,256]{3,2,1,0:T(8,128)(2,1)}) custom-call(s32[1]{0:T(128)} %bitcast.tile_ref, s32[8,8192]{1,0:T(8,128)} %bins_ref.1, f32[8,2,2,15,64]{4,3,2,1,0:T(8,128)} %copy.6.table_ref, ...), custom_call_target="tpu_custom_call" | custom-call | flops 200000000 | bytes 3200000 | tf_op jit(solution)/shard_map/prepare/pallas_call | solution.py:121
  17.9 0.0 copy-start.1
  17.9 0.0 copy-start.3
  17.9 3.6 %rcv_inner.1.rest_0_ = f32[2,392,128]{2,1,0:T(8,128)S(1)} custom-call(f32[2,512,128]{2,1,0:T(8,128)S(1)} %get-tuple-element.17.local_ref, bf16[8,672,128]{2,1,0:T(8,128)(2,1)S(1)} %get-tuple-element.15.taps_ref), custom_call_target="tpu_custom_call" | custom-call | flops 2000000000 | bytes 3000000 | tf_op jit(solution)/shard_map/rcv_inner/pallas_call | solution.py:245
  21.5 0.0 collective-permute-done.low_ref
  21.5 0.9 %collective-permute-done.1.high_ref = f32[2,2,56,128]{3,2,1,0:T(8,128)S(1)} collective-permute-done((f32[2,2,56,128]{3,2,1,0:T(8,128)S(1)}, f32[2,2,56,128]{3,2,1,0:T(8,128)S(1)}, u32[]{:S(2)}, u32[]{:S(2)}) %collective-permute-start.1) | collective-permute-done | bytes 114720 | tf_op jit(solution)/shard_map/ppermute | solution.py:544
  22.4 3.7 %rcv_steps.2 = f32[32,2,1,16,128]{4,3,2,1,0:T(8,128)} custom-call(f32[2,512,128]{2,1,0:T(8,128)S(1)} %get-tuple-element.17.local_ref, f32[2,2,56,128]{3,2,1,0:T(8,128)S(1)} %collective-permute-done.low_ref, f32[2,2,56,128]{3,2,1,0:T(8,128)S(1)} %collective-permute-done.1.high_ref, bf16[8,672,128]{2,1,0:T(8,128)(2,1)S(1)} %get-tuple-element.15.taps_ref, ...), custom_call_target="tpu_custom_call" | custom-call | flops 2500000000 | bytes 4000000 | tf_op jit(solution)/shard_map/rcv_steps/pallas_call | solution.py:266
  26.1 7.9 %all-to-all-start.1 = ((f32[32,2,1,16,128]{4,3,2,1,0:T(8,128)}), f32[32,2,1,16,128]{4,3,2,1,0:T(8,128)S(1)}, u32[]{:S(2)}, u32[]{:S(2)}) async-start(f32[32,2,1,16,128]{4,3,2,1,0:T(8,128)} %rcv_steps.2), calls=%async_computation.1 | async-start | bytes 1048576 | tf_op jit(solution)/shard_map/all_to_all | solution.py:549
  34.0 0.0 copy-start
  34.0 1.0 %copy-done = bf16[2,8,48,256]{3,2,1,0:T(8,128)(2,1)S(1)} copy-done((bf16[2,8,48,256]{3,2,1,0:T(8,128)(2,1)S(1)}, bf16[2,8,48,256]{3,2,1,0:T(8,128)(2,1)}, u32[]{:S(2)}) %copy-start) | copy-done | bytes 393240
  35.0 0.0 copy-start.2
  35.0 0.9 %copy-done.2 = s32[8,32,128]{2,1,0:T(8,128)S(1)} copy-done((s32[8,32,128]{2,1,0:T(8,128)S(1)}, s32[8,32,128]{2,1,0:T(8,128)}, u32[]{:S(2)}) %copy-start.2) | copy-done | bytes 131096
  35.9 5.5 %src_taps.1 = (f32[5,8,32,48,128]{4,3,2,1,0:T(8,128)}, f32[8,128]{1,0:T(8,128)}) custom-call(s32[8,32,128]{2,1,0:T(8,128)S(1)} %copy-done.2, bf16[2,8,48,256]{3,2,1,0:T(8,128)(2,1)S(1)} %copy-done), custom_call_target="tpu_custom_call" | custom-call | flops 1200000000 | bytes 13000000 | tf_op jit(solution)/shard_map/src_taps/pallas_call | solution.py:308
  41.5 0.0 copy-start.4
  41.5 0.7 copy-done.4
  42.1 4.7 %rcv_steps.3 = f32[32,2,1,16,128]{4,3,2,1,0:T(8,128)} custom-call(f32[2,512,128]{2,1,0:T(8,128)S(1)} %get-tuple-element.14.local_ref, f32[2,2,56,128]{3,2,1,0:T(8,128)S(1)} %collective-permute-done.low_ref, f32[2,2,56,128]{3,2,1,0:T(8,128)S(1)} %collective-permute-done.1.high_ref, bf16[8,672,128]{2,1,0:T(8,128)(2,1)S(1)} %get-tuple-element.15.taps_ref, ...), custom_call_target="tpu_custom_call" | custom-call | flops 2500000000 | bytes 4000000 | tf_op jit(solution)/shard_map/rcv_steps/pallas_call | solution.py:266
  46.8 4.0 %all-to-all-done.1 = f32[32,2,1,16,128]{4,3,2,1,0:T(8,128)S(1)} async-done(((f32[32,2,1,16,128]{4,3,2,1,0:T(8,128)}), f32[32,2,1,16,128]{4,3,2,1,0:T(8,128)S(1)}, u32[]{:S(2)}, u32[]{:S(2)}) %all-to-all-start.1) | async-done | bytes 524320 | tf_op jit(solution)/shard_map/all_to_all | solution.py:549
  50.8 3.9 %all-to-all-start = ((f32[32,2,1,16,128]{4,3,2,1,0:T(8,128)}), f32[32,2,1,16,128]{4,3,2,1,0:T(8,128)S(1)}, u32[]{:S(2)}, u32[]{:S(2)}) async-start(f32[32,2,1,16,128]{4,3,2,1,0:T(8,128)} %rcv_steps.3), calls=%async_computation | async-start | bytes 1048576 | tf_op jit(solution)/shard_map/all_to_all | solution.py:552
  54.6 0.0 copy-done.1
  54.7 0.0 copy-done.3
  54.7 12.0 %src_steps.2.rest_0_ = f32[2,2,1,16,4096]{4,3,2,1,0:T(8,128)} custom-call(f32[1024,128]{1,0:T(8,128)S(1)} %bitcast.6, s32[8,32,128]{2,1,0:T(8,128)S(1)} %copy-done.3, bf16[2,8,48,256]{3,2,1,0:T(8,128)(2,1)S(1)} %copy-done.1), custom_call_target="tpu_custom_call" | custom-call | flops 3000000000 | bytes 8000000 | tf_op jit(solution)/shard_map/src_steps/pallas_call | solution.py:503
  66.7 4.6 %all-to-all-done = f32[32,2,1,16,128]{4,3,2,1,0:T(8,128)S(1)} async-done(((f32[32,2,1,16,128]{4,3,2,1,0:T(8,128)}), f32[32,2,1,16,128]{4,3,2,1,0:T(8,128)S(1)}, u32[]{:S(2)}, u32[]{:S(2)}) %all-to-all-start) | async-done | bytes 524320 | tf_op jit(solution)/shard_map/all_to_all | solution.py:552
  71.3 10.7 %src_steps.3 = f32[2,2,1,16,4096]{4,3,2,1,0:T(8,128)} custom-call(f32[1024,128]{1,0:T(8,128)S(1)} %bitcast.5, f32[5,8,32,48,128]{4,3,2,1,0:T(8,128)} %get-tuple-element.21.bins_ref, bf16[2,8,48,256]{3,2,1,0:T(8,128)(2,1)S(1)} %copy-done.1, f32[2,2,1,16,4096]{4,3,2,1,0:T(8,128)} %src_steps.2.rest_0_), custom_call_target="tpu_custom_call", output_to_operand_aliasing={{}: (3, {})} | custom-call | flops 3000000000 | bytes 8000000 | tf_op jit(solution)/shard_map/src_steps/pallas_call | solution.py:503
Async XLA Ops:
  1.3 20.2 %collective-permute-start = (f32[2,2,56,128]{3,2,1,0:T(8,128)S(1)}, f32[2,2,56,128]{3,2,1,0:T(8,128)S(1)}, u32[]{:S(2)}, u32[]{:S(2)}) collective-permute-start(f32[2,2,56,128]{3,2,1,0:T(8,128)S(1)} %bitcast.7), channel_id=1, source_target_pairs={{0,1},{1,2},{2,3},{3,4},{4,5},{5,6},{6,7},{7,8},{8,9},{9,10},{10,1... | collective-permute-start | bytes 344072 | tf_op jit(solution)/shard_map/ppermute | solution.py:543
  8.9 13.5 %collective-permute-start.1 = (f32[2,2,56,128]{3,2,1,0:T(8,128)S(1)}, f32[2,2,56,128]{3,2,1,0:T(8,128)S(1)}, u32[]{:S(2)}, u32[]{:S(2)}) collective-permute-start(f32[2,2,56,128]{3,2,1,0:T(8,128)S(1)} %bitcast.8), channel_id=1, source_target_pairs={{1,0},{2,1},{3,2},{4,3},{5,4},{6,5},{7,6},{8,7},{9,8},{10,9},{11,1... | collective-permute-start | bytes 344072 | tf_op jit(solution)/shard_map/ppermute | solution.py:544
  17.9 36.7 %copy-start.1 = (bf16[2,8,48,256]{3,2,1,0:T(8,128)(2,1)S(1)}, bf16[2,8,48,256]{3,2,1,0:T(8,128)(2,1)}, u32[]{:S(2)}) copy-start(bf16[2,8,48,256]{3,2,1,0:T(8,128)(2,1)} %get-tuple-element.19.table_ref) | copy-start | bytes 1179652
  17.9 36.7 %copy-start.3 = (s32[8,32,128]{2,1,0:T(8,128)S(1)}, s32[8,32,128]{2,1,0:T(8,128)}, u32[]{:S(2)}) copy-start(s32[8,32,128]{2,1,0:T(8,128)} %get-tuple-element.18.bins_ref) | copy-start | bytes 393220
  26.1 24.7 %all-to-all-start.1 = ((f32[32,2,1,16,128]{4,3,2,1,0:T(8,128)}), f32[32,2,1,16,128]{4,3,2,1,0:T(8,128)S(1)}, u32[]{:S(2)}, u32[]{:S(2)}) async-start(f32[32,2,1,16,128]{4,3,2,1,0:T(8,128)} %rcv_steps.2), calls=%async_computation.1 | async-start | bytes 1048576 | tf_op jit(solution)/shard_map/all_to_all | solution.py:549
  34.0 1.0 %copy-start = (bf16[2,8,48,256]{3,2,1,0:T(8,128)(2,1)S(1)}, bf16[2,8,48,256]{3,2,1,0:T(8,128)(2,1)}, u32[]{:S(2)}) copy-start(bf16[2,8,48,256]{3,2,1,0:T(8,128)(2,1)} %get-tuple-element.19.table_ref) | copy-start | bytes 1179652
  35.0 0.9 %copy-start.2 = (s32[8,32,128]{2,1,0:T(8,128)S(1)}, s32[8,32,128]{2,1,0:T(8,128)}, u32[]{:S(2)}) copy-start(s32[8,32,128]{2,1,0:T(8,128)} %get-tuple-element.18.bins_ref) | copy-start | bytes 393220
  41.5 0.7 copy-start.4
  50.8 20.5 %all-to-all-start = ((f32[32,2,1,16,128]{4,3,2,1,0:T(8,128)}), f32[32,2,1,16,128]{4,3,2,1,0:T(8,128)S(1)}, u32[]{:S(2)}, u32[]{:S(2)}) async-start(f32[32,2,1,16,128]{4,3,2,1,0:T(8,128)} %rcv_steps.3), calls=%async_computation | async-start | bytes 1048576 | tf_op jit(solution)/shard_map/all_to_all | solution.py:552
